TPU v7x, 32 devices: a whole 2x2x4 slice. The times are simulated.
32 devices in a mesh: node: 8 (over z, y), local: 4 (over x, core).
Axes of the slice: x: 2, y: 2, z: 4, core: 2. Of those that a mesh axis runs over, the one named last changes fastest.
Arguments:
- tokens: bfloat16 [4096, 4096], P(('node', 'local')), may hold values from -6 to 6
- key_codes: bfloat16 [4096, 512], P('local'), may hold values from -0.09375 to 0.09375
- key_exponents: int32 [4096, 2], P('local'), may hold values from -1 to 1
- key_cotangent: bfloat16 [4096, 512], P(('node', 'local')), may hold values from -6 to 6
Outputs:
- keys: bfloat16 [4096, 512], P(('node', 'local'))
- input_grad: bfloat16 [4096, 4096], P(('node', 'local'))
- weight_grad: float32 [4096, 512], P(('node', 'local'))
Inputs may be any that keep to these rules, and one draw needn't show every extreme that they name: key_exponents gives the power of two that scales each block of 256 columns of a row of key_codes.
All inputs are finite; a program needn't handle non-finite values.
Results may differ from a plain program's by a relative error of at most 0.015.
Values may be sent and summed in bfloat16 or wider, within the bound.
A program may use at most 128 MiB of HBM per device.

v0:
```python
import functools
import math

import jax
import jax.numpy as jnp
import numpy as np
from jax import lax
from jax.experimental import pallas as pl
from jax.experimental.pallas import tpu as pltpu
from jax.sharding import PartitionSpec as P

KVH = 4
HEAD = 128
QBLOCK = 256
SEQ = 8192
MESH = pl.DeviceIdType.MESH


THETA = 500000.0


def tables(positions):
    inverse = THETA ** (-(jnp.arange(HEAD // 2, dtype=jnp.float32) * 2.0 / HEAD))
    angles = positions.astype(jnp.float32)[:, None] * inverse[None, :]
    return (jnp.cos(angles), jnp.sin(angles))


def rotate(values, cosine, sine_part):
    count = values.shape[0]
    heads = values.reshape(count, KVH, HEAD)
    first_half = heads[:, :, : HEAD // 2]
    second_half = heads[:, :, HEAD // 2 :]
    cos_rows = cosine[:, None, :]
    sin_rows = sine_part[:, None, :]
    joined = jnp.concatenate(
        [
            first_half * cos_rows - second_half * sin_rows,
            second_half * cos_rows + first_half * sin_rows,
        ],
        axis=2,
    )
    return joined.reshape(count, KVH * HEAD)


def unrotate(values, cosine, sine_part):
    count = values.shape[0]
    heads = values.reshape(count, KVH, HEAD)
    first_half = heads[:, :, : HEAD // 2]
    second_half = heads[:, :, HEAD // 2 :]
    cos_rows = cosine[:, None, :]
    sin_rows = sine_part[:, None, :]
    joined = jnp.concatenate(
        [
            first_half * cos_rows + second_half * sin_rows,
            second_half * cos_rows - first_half * sin_rows,
        ],
        axis=2,
    )
    return joined.reshape(count, KVH * HEAD)


def quantize(partial_value):
    blocks = partial_value.reshape(partial_value.shape[0], partial_value.shape[1] // QBLOCK, QBLOCK)
    largest = jnp.max(jnp.abs(blocks), axis=2)
    block_scale = jnp.exp2(jnp.ceil(jnp.log2(largest + 1e-06)))
    code_values = (blocks / block_scale[:, :, None]).astype(jnp.bfloat16)
    return (code_values, block_scale.astype(jnp.bfloat16))


def expand_codes(code_values, block_scale):
    lead = code_values.shape[:-1]
    blocks = code_values.reshape(lead + (block_scale.shape[-1], QBLOCK))
    values = blocks.astype(jnp.float32) * block_scale.astype(jnp.float32)[..., None]
    return values.reshape(lead + (code_values.shape[-1],))


def on_device(tokens, key_codes, key_exponents, key_cotangent):
    node_count = lax.axis_size("node")
    local_count = lax.axis_size("local")
    tok_count = tokens.shape[0]
    width = tokens.shape[1]
    feature_count = key_codes.shape[1]
    expanded = jnp.repeat(jnp.exp2(key_exponents.astype(jnp.float32)), QBLOCK, axis=1)
    shard_weights = (key_codes.astype(jnp.float32) * expanded).astype(jnp.bfloat16)
    weights = lax.all_gather(shard_weights, "local", axis=0, tiled=True)
    device_index = lax.axis_index("node") * local_count + lax.axis_index("local")
    positions = (device_index * tok_count + jnp.arange(tok_count, dtype=jnp.int32)) % SEQ
    cosine, sine_part = tables(positions)
    pre_grad = unrotate(key_cotangent.astype(jnp.float32), cosine, sine_part).astype(jnp.bfloat16)
    partial_value = lax.dot_general(
        tokens, pre_grad, (((0,), (0,)), ((), ())), preferred_element_type=jnp.float32
    )
    code_values, block_scale = quantize(partial_value)
    row_count = width // (node_count * local_count)
    block_count = feature_count // QBLOCK
    code_grid = code_values.reshape(node_count, local_count, row_count, feature_count)
    scale_grid = block_scale.reshape(node_count, local_count, row_count, block_count)
    projected = jnp.dot(tokens, weights, preferred_element_type=jnp.float32)
    keys = rotate(projected, cosine, sine_part).astype(jnp.bfloat16)
    input_grad = lax.dot_general(
        pre_grad, weights, (((1,), (1,)), ((), ())), preferred_element_type=jnp.float32
    ).astype(jnp.bfloat16)
    got_codes, got_scales = (
        lax.all_to_all(code_grid, "local", split_axis=1, concat_axis=1, tiled=True),
        lax.all_to_all(scale_grid, "local", split_axis=1, concat_axis=1, tiled=True),
    )
    node_terms = jnp.sum(expand_codes(got_codes, got_scales), axis=1)
    summed = (
        lax.psum_scatter(node_terms.astype(jnp.bfloat16), "node", scatter_dimension=0, tiled=True)
        .astype(jnp.float32)
        .reshape(row_count, feature_count)
    )
    total_tokens = tok_count * node_count * local_count
    weight_grad = summed * (1.0 / math.sqrt(total_tokens))
    return (keys, input_grad, weight_grad)


def flip(index, distance):
    result = index
    bit = 1
    while bit <= distance:
        if distance & bit:
            result = result + bit - 2 * bit * lax.rem(lax.div(index, bit), 2)
        bit *= 2
    return result


def turn(values, cosine, signed_sine):
    parts = []
    for head in range(values.shape[1] // HEAD):
        piece = values[:, head * HEAD : (head + 1) * HEAD]
        parts.append(piece * cosine + pltpu.roll(piece, HEAD // 2, 1) * signed_sine)
    return jnp.concatenate(parts, axis=1)


def fused_kernel(
    nodes,
    locals_,
    chunks,
    tokens_hbm,
    codes_hbm,
    exponents_ref,
    cotangent_ref,
    inverse_ref,
    keys_ref,
    input_grad_ref,
    weight_grad_ref,
    tokens,
    codes,
    columns,
    pre,
    weights,
    outgoing,
    incoming,
    kept,
    load_sem,
    own_sem,
    column_send,
    column_recv,
    pre_send,
    pre_recv,
    weight_send,
    across_send,
    weight_recv,
    sum_send,
    sum_recv,
):
    node = lax.axis_index("node")
    local = lax.axis_index("local")
    count = tokens.shape[0]
    row_count = columns.shape[2]
    shard_rows = weights.shape[1]
    chunk_rows = shard_rows // chunks
    total = count * nodes * locals_

    barrier = pltpu.get_barrier_semaphore()
    for d in range(1, locals_):
        pl.semaphore_signal(barrier, inc=1, device_id=(node, flip(local, d)), device_id_type=MESH)
    reached = [1] + list(range(2, nodes, 2))
    for e in reached:
        pl.semaphore_signal(barrier, inc=1, device_id=(flip(node, e), local), device_id_type=MESH)

    load_codes = pltpu.make_async_copy(codes_hbm, codes, load_sem.at[0])
    load_codes.start()
    load_tokens = pltpu.make_async_copy(tokens_hbm, tokens, load_sem.at[1])
    load_tokens.start()

    def owned(e, d):
        first = (flip(node, e) * locals_ + flip(local, d)) * row_count
        return pl.ds(pl.multiple_of(first, row_count), row_count)

    order = list(range(nodes - 1, -1, -1))
    own = {}
    for e in order:
        own[e] = pltpu.make_async_copy(
            tokens_hbm.at[:, owned(e, 0)], columns.at[e, pl.ds(0, count), :], own_sem.at[e]
        )
        own[e].start()

    start = lax.rem((node * locals_ + local) * count, SEQ)
    positions = lax.rem(start + lax.broadcasted_iota(jnp.int32, (count, HEAD), 0), SEQ)
    angles = positions.astype(jnp.float32) * inverse_ref[...]
    cosine = jnp.cos(angles)
    sine = jnp.sin(angles)
    lane = lax.broadcasted_iota(jnp.int32, (count, HEAD), 1)
    signed_sine = jnp.where(lane < HEAD // 2, -sine, sine)
    pre[pl.ds(0, count), :] = turn(
        cotangent_ref[...].astype(jnp.float32), cosine, -signed_sine
    ).astype(jnp.bfloat16)

    pl.semaphore_wait(barrier, locals_ - 1 + len(reached))

    sends = []

    def send_pre(source, slot, distance):
        copy = pltpu.make_async_remote_copy(
            src_ref=pre.at[pl.ds(source * count, count), :],
            dst_ref=pre.at[pl.ds(slot * count, count), :],
            send_sem=pre_send.at[slot],
            recv_sem=pre_recv.at[slot],
            device_id=(node, flip(local, distance)),
            device_id_type=MESH,
        )
        copy.start()
        sends.append(copy)
        return copy

    pre_copies = {d: send_pre(0, d, d) for d in range(2, locals_, 2)}
    pre_copies[1] = send_pre(0, 1, 1)
    column_copies = {}
    for e in order:
        for d in range(locals_ - 1, 0, -1):
            copy = pltpu.make_async_remote_copy(
                src_ref=tokens_hbm.at[:, owned(e, d)],
                dst_ref=columns.at[e, pl.ds(d * count, count), :],
                send_sem=column_send.at[e, d],
                recv_sem=column_recv.at[e, d],
                device_id=(node, flip(local, d)),
                device_id_type=MESH,
            )
            copy.start()
            column_copies[e, d] = copy
            sends.append(copy)

    halves = [lax.rem(node, 2), lax.rem(lax.div(node, 2), 2)]

    def rows_of(turn_at, via):
        half = halves[turn_at % 2]
        part = turn_at * 2 + (1 - half if via else half)
        return pl.ds(pl.multiple_of(part * chunk_rows, chunk_rows), chunk_rows)

    def send_weights(source, slot, turn_at, via, device, kind, landing):
        copy = pltpu.make_async_remote_copy(
            src_ref=weights.at[source, rows_of(turn_at, via), :],
            dst_ref=weights.at[slot, rows_of(turn_at, via), :],
            send_sem=kind.at[slot, turn_at, via],
            recv_sem=weight_recv.at[slot, turn_at, landing],
            device_id=device,
            device_id_type=MESH,
        )
        copy.start()
        sends.append(copy)
        return copy

    partner = (node, flip(local, 1))
    across = [(flip(node, 1), local), (flip(node, 2), local)]
    turns = chunks // 2
    load_codes.wait()
    scale = jnp.left_shift(1, exponents_ref[...] + 15).astype(jnp.float32) * (2.0**-15)
    scale = jnp.transpose(jnp.concatenate([scale] * (8 // scale.shape[0]), axis=0))
    for block in range(codes.shape[1] // QBLOCK):
        lanes = pl.ds(block * QBLOCK, QBLOCK)
        weights[0, :, lanes] = (
            codes[:, lanes].astype(jnp.float32) * scale[:, block : block + 1]
        ).astype(jnp.bfloat16)
    arrivals = {}
    for turn_at in range(turns):
        for d in range(2, locals_, 2):
            device = (node, flip(local, d))
            arrivals[d, turn_at, 0] = send_weights(0, d, turn_at, 0, device, weight_send, 0)
        for via in range(2):
            arrivals[1, turn_at, via] = send_weights(0, 1, turn_at, via, partner, weight_send, via)

    for d in range(2, locals_, 2):
        pre_copies[d].wait_recv()
        pre_copies[d + 1] = send_pre(d, d + 1, 1)
    pre_copies[1].wait_recv()
    for d in range(3, locals_, 2):
        pre_copies[d].wait_recv()
    load_tokens.wait()
    projected = jnp.zeros((count, weights.shape[2]), jnp.float32)

    def use(slot, turn_at, via, projected):
        rows = rows_of(turn_at, via)
        first = flip(local, slot) * shard_rows + rows.start
        lanes = pl.ds(pl.multiple_of(first, chunk_rows), chunk_rows)
        block = weights[slot, rows, :]
        input_grad_ref[:, lanes] = lax.dot_general(
            pre[pl.ds(0, count), :],
            block,
            (((1,), (1,)), ((), ())),
            preferred_element_type=jnp.float32,
        ).astype(jnp.bfloat16)
        return projected + jnp.dot(tokens[:, lanes], block, preferred_element_type=jnp.float32)

    def late(turn_at, projected):
        for d in range(2, locals_, 2):
            arrivals[d, turn_at, 1].wait_recv()
            arrivals[d + 1, turn_at, 1] = send_weights(
                d, d + 1, turn_at, 1, partner, weight_send, 1
            )
            projected = use(d, turn_at, 1, projected)
        for d in range(3, locals_, 2):
            arrivals[d, turn_at, 1].wait_recv()
            projected = use(d, turn_at, 1, projected)
        return projected

    early = [(0, t, v) for t in range(turns) for v in range(2)]
    early += [(1, t, v) for t in range(turns) for v in range(2)]
    sum_copies = {}

    def send_sum(e, value, device):
        outgoing[e] = value.astype(jnp.bfloat16)
        copy = pltpu.make_async_remote_copy(
            src_ref=outgoing.at[e],
            dst_ref=incoming.at[e],
            send_sem=sum_send.at[e],
            recv_sem=sum_recv.at[e],
            device_id=device,
            device_id_type=MESH,
        )
        copy.start()
        sends.append(copy)
        return copy

    def finish(pair):
        sum_copies[2 * pair + 1].wait_recv()
        value = kept[pair] + incoming[2 * pair + 1].astype(jnp.float32)
        if pair:
            sum_copies[2 * pair] = send_sum(2 * pair, value, (flip(node, 2 * pair), local))
        else:
            kept[0] = value

    for e in order:
        own[e].wait()
        for d in range(1, locals_):
            column_copies[e, d].wait_recv()
        piece = lax.dot_general(
            columns[e], pre[...], (((0,), (0,)), ((), ())), preferred_element_type=jnp.float32
        )
        if e % 2 == 1:
            sum_copies[e] = send_sum(e, piece, (flip(node, 1), local))
        else:
            kept[e // 2] = piece
            if e + 2 < nodes:
                finish(e // 2 + 1)
        for _ in range(min(2, len(early))):
            slot, turn_at, via = early.pop(0)
            if slot == 1:
                arrivals[1, turn_at, via].wait_recv()
            projected = use(slot, turn_at, via, projected)

    for slot, turn_at, via in early:
        if slot == 1:
            arrivals[1, turn_at, via].wait_recv()
        projected = use(slot, turn_at, via, projected)
    for turn_at in range(turns):
        for d in range(2, locals_, 2):
            arrivals[d, turn_at, 0].wait_recv()
            arrivals[d, turn_at, 1] = send_weights(
                d, d, turn_at, 0, across[turn_at % 2], across_send, 1
            )
            arrivals[d + 1, turn_at, 0] = send_weights(
                d, d + 1, turn_at, 0, partner, weight_send, 0
            )
            projected = use(d, turn_at, 0, projected)
        for d in range(3, locals_, 2):
            arrivals[d, turn_at, 0].wait_recv()
            projected = use(d, turn_at, 0, projected)
        if turn_at == 0:
            finish(0)
        else:
            projected = late(turn_at - 1, projected)
    projected = late(turns - 1, projected)
    keys_ref[...] = turn(projected, cosine, signed_sine).astype(jnp.bfloat16)

    summed = kept[0]
    for e in range(nodes - 2, 0, -2):
        sum_copies[e].wait_recv()
        summed = summed + incoming[e].astype(jnp.float32)
    weight_grad_ref[...] = summed * (1.0 / math.sqrt(total))
    for copy in sends:
        copy.wait_send()


def fused(tokens, key_codes, key_exponents, key_cotangent):
    nodes = lax.axis_size("node")
    locals_ = lax.axis_size("local")
    count, width = tokens.shape
    features = key_codes.shape[1]
    shard_rows = key_codes.shape[0]
    row_count = width // (nodes * locals_)
    chunks = 8
    half = THETA ** (-(np.arange(HEAD // 2) * 2.0 / HEAD))
    inverse = jnp.asarray(np.concatenate([half, half])[None, :], jnp.float32)
    anywhere = pl.BlockSpec(memory_space=pl.ANY)
    vmem = pl.BlockSpec(memory_space=pltpu.VMEM)
    dma = pltpu.SemaphoreType.DMA
    return pl.pallas_call(
        functools.partial(fused_kernel, nodes, locals_, chunks),
        out_shape=(
            pltpu.VMEM((count, features), jnp.bfloat16),
            pltpu.VMEM((count, width), jnp.bfloat16),
            pltpu.VMEM((row_count, features), jnp.float32),
        ),
        in_specs=[anywhere, anywhere, vmem, vmem, vmem],
        out_specs=(vmem, vmem, vmem),
        scratch_shapes=[
            pltpu.VMEM((count, width), jnp.bfloat16),
            pltpu.VMEM((shard_rows, features), jnp.bfloat16),
            pltpu.VMEM((nodes, locals_ * count, row_count), jnp.bfloat16),
            pltpu.VMEM((locals_ * count, features), jnp.bfloat16),
            pltpu.VMEM((locals_, shard_rows, features), jnp.bfloat16),
            pltpu.VMEM((nodes, row_count, features), jnp.bfloat16),
            pltpu.VMEM((nodes, row_count, features), jnp.bfloat16),
            pltpu.VMEM((nodes // 2, row_count, features), jnp.float32),
            dma((2,)),
            dma((nodes,)),
            dma((nodes, locals_)),
            dma((nodes, locals_)),
            dma((locals_,)),
            dma((locals_,)),
            dma((locals_, chunks // 2, 2)),
            dma((locals_, chunks // 2, 2)),
            dma((locals_, chunks // 2, 2)),
            dma((nodes,)),
            dma((nodes,)),
        ],
        compiler_params=pltpu.CompilerParams(collective_id=0, has_side_effects=True),
    )(tokens, key_codes, key_exponents.T, key_cotangent, inverse)


def solution(mesh):
    def body(tokens, key_codes, key_exponents, key_cotangent):
        row_count = tokens.shape[1] // (mesh.shape["node"] * mesh.shape["local"])
        even = mesh.shape["node"] % 4 == 0 and mesh.shape["local"] % 2 == 0
        run = fused if even and row_count % HEAD == 0 else on_device
        return run(tokens, key_codes, key_exponents, key_cotangent)

    return jax.shard_map(
        body,
        mesh=mesh,
        in_specs=(
            P(("node", "local"), None),
            P("local", None),
            P("local", None),
            P(("node", "local"), None),
        ),
        out_specs=(
            P(("node", "local"), None),
            P(("node", "local"), None),
            P(("node", "local"), None),
        ),
        check_vma=False,
    )
```

profile of v0, /device:TPU:0, one launch (start us, length us, event | category | flops | bytes accessed | tf_op | source)
XLA Modules:
  0.0 44.9 jit_solution(7211165451518635136)
XLA Ops:
  0.6 41.9 %shard_map.76 = (bf16[128,512]{1,0:T(8,128)(2,1)S(1)}, bf16[128,4096]{1,0:T(8,128)(2,1)S(1)}, f32[128,512]{1,0:T(8,128)S(1)}) custom-call(bf16[128,4096]{1,0:T(8,128)(2,1)} %tokens_hbm.1, bf16[1024,512]{1,0:T(8,128)(2,1)} %codes_hbm.1, s32[2,1024]{1,0:T(2,128)} %bitcast.1, bf16[128,512]{1,0:T(8,128)(2,1)} %cotangent_ref.1, f32[1,128]{1,0:T(1,128)} %constant.2.clone.inverse_ref), custom_call_target="tpu_custom_call" | custom-call | tf_op jit(solution)/shard_map/pallas_call | solution.py:409
  42.5 0.7 %copy.11 = bf16[128,512]{1,0:T(8,128)(2,1)} copy(bf16[128,512]{1,0:T(8,128)(2,1)S(1)} %get-tuple-element.3) | data formatting | bytes 262144
  43.2 0.7 %copy.13 = f32[128,512]{1,0:T(8,128)} copy(f32[128,512]{1,0:T(8,128)S(1)} %get-tuple-element.5) | data formatting | bytes 524288
  43.9 1.0 %copy.12 = bf16[128,4096]{1,0:T(8,128)(2,1)} copy(bf16[128,4096]{1,0:T(8,128)(2,1)S(1)} %get-tuple-element.4) | data formatting | bytes 2097152
where the time goes:
time: 45.1 us; the launch traced here: 44.9 us
  Pallas kernels  41.9 us (93%)
  local copies, waits for them, and re-layouts  2.33 us (5%)
  between operations  0.64 us (1%)
    pallas_call x1, Pallas kernels, fused(): pl.pallas_call(functools.partial(fused_kernel, nodes, locals_, chunks), o...  41.9 us
    unnamed x3, local copies, waits for them, and re-layouts  2.33 us

commit v1 on v0

v1 whole, which is shorter than its diff:
```python
import functools
import math

import jax
import jax.numpy as jnp
import numpy as np
from jax import lax
from jax.experimental import pallas as pl
from jax.experimental.pallas import tpu as pltpu
from jax.sharding import PartitionSpec as P

KVH = 4
HEAD = 128
QBLOCK = 256
SEQ = 8192
MESH = pl.DeviceIdType.MESH


THETA = 500000.0


def tables(positions):
    inverse = THETA ** (-(jnp.arange(HEAD // 2, dtype=jnp.float32) * 2.0 / HEAD))
    angles = positions.astype(jnp.float32)[:, None] * inverse[None, :]
    return (jnp.cos(angles), jnp.sin(angles))


def rotate(values, cosine, sine_part):
    count = values.shape[0]
    heads = values.reshape(count, KVH, HEAD)
    first_half = heads[:, :, : HEAD // 2]
    second_half = heads[:, :, HEAD // 2 :]
    cos_rows = cosine[:, None, :]
    sin_rows = sine_part[:, None, :]
    joined = jnp.concatenate(
        [
            first_half * cos_rows - second_half * sin_rows,
            second_half * cos_rows + first_half * sin_rows,
        ],
        axis=2,
    )
    return joined.reshape(count, KVH * HEAD)


def unrotate(values, cosine, sine_part):
    count = values.shape[0]
    heads = values.reshape(count, KVH, HEAD)
    first_half = heads[:, :, : HEAD // 2]
    second_half = heads[:, :, HEAD // 2 :]
    cos_rows = cosine[:, None, :]
    sin_rows = sine_part[:, None, :]
    joined = jnp.concatenate(
        [
            first_half * cos_rows + second_half * sin_rows,
            second_half * cos_rows - first_half * sin_rows,
        ],
        axis=2,
    )
    return joined.reshape(count, KVH * HEAD)


def quantize(partial_value):
    blocks = partial_value.reshape(partial_value.shape[0], partial_value.shape[1] // QBLOCK, QBLOCK)
    largest = jnp.max(jnp.abs(blocks), axis=2)
    block_scale = jnp.exp2(jnp.ceil(jnp.log2(largest + 1e-06)))
    code_values = (blocks / block_scale[:, :, None]).astype(jnp.bfloat16)
    return (code_values, block_scale.astype(jnp.bfloat16))


def expand_codes(code_values, block_scale):
    lead = code_values.shape[:-1]
    blocks = code_values.reshape(lead + (block_scale.shape[-1], QBLOCK))
    values = blocks.astype(jnp.float32) * block_scale.astype(jnp.float32)[..., None]
    return values.reshape(lead + (code_values.shape[-1],))


def on_device(tokens, key_codes, key_exponents, key_cotangent):
    node_count = lax.axis_size("node")
    local_count = lax.axis_size("local")
    tok_count = tokens.shape[0]
    width = tokens.shape[1]
    feature_count = key_codes.shape[1]
    expanded = jnp.repeat(jnp.exp2(key_exponents.astype(jnp.float32)), QBLOCK, axis=1)
    shard_weights = (key_codes.astype(jnp.float32) * expanded).astype(jnp.bfloat16)
    weights = lax.all_gather(shard_weights, "local", axis=0, tiled=True)
    device_index = lax.axis_index("node") * local_count + lax.axis_index("local")
    positions = (device_index * tok_count + jnp.arange(tok_count, dtype=jnp.int32)) % SEQ
    cosine, sine_part = tables(positions)
    pre_grad = unrotate(key_cotangent.astype(jnp.float32), cosine, sine_part).astype(jnp.bfloat16)
    partial_value = lax.dot_general(
        tokens, pre_grad, (((0,), (0,)), ((), ())), preferred_element_type=jnp.float32
    )
    code_values, block_scale = quantize(partial_value)
    row_count = width // (node_count * local_count)
    block_count = feature_count // QBLOCK
    code_grid = code_values.reshape(node_count, local_count, row_count, feature_count)
    scale_grid = block_scale.reshape(node_count, local_count, row_count, block_count)
    projected = jnp.dot(tokens, weights, preferred_element_type=jnp.float32)
    keys = rotate(projected, cosine, sine_part).astype(jnp.bfloat16)
    input_grad = lax.dot_general(
        pre_grad, weights, (((1,), (1,)), ((), ())), preferred_element_type=jnp.float32
    ).astype(jnp.bfloat16)
    got_codes, got_scales = (
        lax.all_to_all(code_grid, "local", split_axis=1, concat_axis=1, tiled=True),
        lax.all_to_all(scale_grid, "local", split_axis=1, concat_axis=1, tiled=True),
    )
    node_terms = jnp.sum(expand_codes(got_codes, got_scales), axis=1)
    summed = (
        lax.psum_scatter(node_terms.astype(jnp.bfloat16), "node", scatter_dimension=0, tiled=True)
        .astype(jnp.float32)
        .reshape(row_count, feature_count)
    )
    total_tokens = tok_count * node_count * local_count
    weight_grad = summed * (1.0 / math.sqrt(total_tokens))
    return (keys, input_grad, weight_grad)


def flip(index, distance):
    result = index
    bit = 1
    while bit <= distance:
        if distance & bit:
            result = result + bit - 2 * bit * lax.rem(lax.div(index, bit), 2)
        bit *= 2
    return result


def turn(values, cosine, signed_sine):
    parts = []
    for head in range(values.shape[1] // HEAD):
        piece = values[:, head * HEAD : (head + 1) * HEAD]
        parts.append(piece * cosine + pltpu.roll(piece, HEAD // 2, 1) * signed_sine)
    return jnp.concatenate(parts, axis=1)


CORES = 2
DEPTH = 4
GROUPS = ("S1", "P2z", "P2z")
ROUTES = {
    "S1": {
        (0, 0): ("x", {"z": (1, 0), "y": (0, 1)}),
        (1, 0): ("z", {"y": (1, 1)}),
        (0, 1): ("y", {}),
        (1, 1): ("y", {}),
    },
    "S2": {
        (0, 0): ("x", {"y": (0, 1), "z": (1, 0)}),
        (0, 1): ("y", {"z": (1, 1)}),
        (1, 0): ("z", {}),
        (1, 1): ("z", {}),
    },
    "P2z": {(0, 0): ("x", {"z": (1, 0)}), (1, 0): ("z", {})},
    "P2y": {(0, 0): ("x", {"y": (0, 1)}), (0, 1): ("y", {})},
}
SIZES = {"S1": 4, "S2": 4, "P2z": 2, "P2y": 2}
ORDER = (
    "xw0:00", "ypre", "cpre", "yc3f", "ccols", "cw", "yc2f", "yc3n", "xw1:00", "yc1f", "yc2n", "yc0f", "yc1n",
    "o0", "o1", "o2", "o3",
    "w0:00",
    "rpre",
    "p0", "p1",
    "g3f", "xw2:00",
    "w1:00", "p2",
    "g2f", "p3",
    "g3n", "u0:00", "v0:00",
    "w0:10", "g1f", "g2n",
    "u1:00", "v1:00",
    "s3",
    "g0f", "g1n",
    "w1:10", "w2:00", "u0:10", "v0:10",
    "u1:10", "v1:10", "u2:00", "v2:00",
    "yc0n",
    "w2:10",
    "s2", "s1",
    "u2:10", "v2:10",
    "w0:01", "u0:01", "v0:01",
    "w0:11", "g0n", "u0:11", "v0:11",
    "fin",
)


def fused_kernel(
    tokens_hbm,
    codes_hbm,
    exponents_ref,
    cotangent_ref,
    inverse_ref,
    keys_ref,
    input_grad_ref,
    weight_grad_ref,
    tokens,
    codes,
    columns,
    pre,
    weights,
    out_x,
    in_x,
    out_z,
    in_z,
    kept,
    projected,
    load_sem,
    own_sem,
    column_send,
    column_recv,
    pre_send,
    pre_recv,
    own_send,
    own_recv,
    weight_send,
    weight_recv,
    sum_send,
    sum_recv,
):
    node = lax.axis_index("node")
    local = lax.axis_index("local")
    nodes = lax.axis_size("node")
    locals_ = lax.axis_size("local")
    count = tokens.shape[0]
    row_count = columns.shape[2]
    shard_rows = weights.shape[1]
    unit_rows = shard_rows // sum(SIZES[g] for g in GROUPS)
    total = count * nodes * locals_

    peers = {
        "c": (node, flip(local, 1)),
        "x": (node, flip(local, 2)),
        "y": (flip(node, 1), local),
        "d": (flip(node, 1), flip(local, 1)),
        "z": (flip(node, 2), local),
        "f": (flip(node, 4), local),
    }
    barrier = pltpu.get_barrier_semaphore()
    for peer in peers.values():
        pl.semaphore_signal(barrier, inc=1, device_id=peer, device_id_type=MESH)

    load_codes = pltpu.make_async_copy(codes_hbm, codes, load_sem.at[0])
    load_codes.start()
    load_tokens = pltpu.make_async_copy(tokens_hbm, tokens, load_sem.at[1])
    load_tokens.start()

    def owned(r, far, e=0, d=0):
        first = (flip(node, 2 * r + e) * locals_ + flip(local, 2 * far + d)) * row_count
        return pl.ds(pl.multiple_of(first, row_count), row_count)

    def slot_rows(slot):
        return pl.ds(slot * count, count)

    own = {}
    for r in range(DEPTH):
        for far in range(2):
            k = 2 * r + far
            own[k] = pltpu.make_async_copy(
                tokens_hbm.at[:, owned(r, far)], columns.at[k, slot_rows(0), :], own_sem.at[k]
            )
            own[k].start()

    start = lax.rem((node * locals_ + local) * count, SEQ)
    positions = lax.rem(start + lax.broadcasted_iota(jnp.int32, (count, HEAD), 0), SEQ)
    angles = positions.astype(jnp.float32) * inverse_ref[...]
    cosine = jnp.cos(angles)
    sine = jnp.sin(angles)
    lane = lax.broadcasted_iota(jnp.int32, (count, HEAD), 1)
    signed_sine = jnp.where(lane < HEAD // 2, -sine, sine)
    pre[slot_rows(0), :] = turn(
        cotangent_ref[...].astype(jnp.float32), cosine, -signed_sine
    ).astype(jnp.bfloat16)

    load_codes.wait()
    scale = jnp.left_shift(1, exponents_ref[...] + 15).astype(jnp.float32) * (2.0**-15)
    scale = jnp.transpose(jnp.concatenate([scale] * (8 // scale.shape[0]), axis=0))
    for block in range(codes.shape[1] // QBLOCK):
        lanes = pl.ds(block * QBLOCK, QBLOCK)
        weights[0, :, lanes] = (
            codes[:, lanes].astype(jnp.float32) * scale[:, block : block + 1]
        ).astype(jnp.bfloat16)
    load_tokens.wait()
    projected[...] = jnp.zeros_like(projected)

    sends = []

    def send(src, dst, send_sem, recv_sem, peer):
        copy = pltpu.make_async_remote_copy(
            src_ref=src,
            dst_ref=dst,
            send_sem=send_sem,
            recv_sem=recv_sem,
            device_id=peers[peer],
            device_id_type=MESH,
        )
        copy.start()
        sends.append(copy)
        return copy

    waits = {}

    def send_columns(name, slot, peer, r, far, e, d):
        k = 2 * r + far
        waits[name, k] = send(
            tokens.at[:, owned(r, far, e, d)],
            columns.at[k, slot_rows(slot), :],
            column_send.at[k, slot],
            column_recv.at[k, slot],
            peer,
        )

    def send_pre(source, slot, peer):
        waits["pre", slot] = send(
            pre.at[slot_rows(source), :],
            pre.at[slot_rows(slot), :],
            pre_send.at[slot],
            pre_recv.at[slot],
            peer,
        )

    blocks = 4
    block_rows = shard_rows // blocks

    def use(slot, first, length):
        rows = pl.ds(pl.multiple_of(first, length), length)
        lane_first = flip(local, slot) * shard_rows + first
        lanes = pl.ds(pl.multiple_of(lane_first, length), length)
        block = weights[slot, rows, :]
        input_grad_ref[:, lanes] = lax.dot_general(
            pre[slot_rows(0), :],
            block,
            (((1,), (1,)), ((), ())),
            preferred_element_type=jnp.float32,
        ).astype(jnp.bfloat16)
        projected[...] += jnp.dot(
            tokens[:, lanes], block, preferred_element_type=jnp.float32
        )

    zbit = lax.rem(lax.div(node, 2), 2)
    ybit = lax.rem(node, 2)
    bases = [sum(SIZES[g] for g in GROUPS[:i]) for i in range(len(GROUPS))]

    def unit_first(group, key):
        kind = GROUPS[group]
        dz, dy = key
        zz = 1 - zbit if dz else zbit
        yy = 1 - ybit if dy else ybit
        index = {"S1": 2 * zz + yy, "S2": 2 * zz + yy, "P2z": zz, "P2y": yy}[kind]
        return pl.multiple_of((bases[group] + index) * unit_rows, unit_rows)

    def sem_index(group, key):
        kind = GROUPS[group]
        dz, dy = key
        return bases[group] + {"S1": 2 * dz + dy, "S2": 2 * dz + dy, "P2z": dz, "P2y": dy}[kind]

    def send_unit(source, slot, group, source_key, key, peer):
        rows = pl.ds(unit_first(group, source_key), unit_rows)
        lane_of = {"x": 0, "y": 1, "z": 2, "c": 3}[peer]
        waits["w", slot, group, key] = send(
            weights.at[source, rows, :],
            weights.at[slot, rows, :],
            weight_send.at[lane_of, sem_index(group, source_key)],
            weight_recv.at[slot - 2, sem_index(group, key)],
            peer,
        )

    def piece(r, far):
        k = 2 * r + far
        own[k].wait()
        for name in "cyd":
            waits[name, k].wait_recv()
        return lax.dot_general(
            columns[k], pre[...], (((0,), (0,)), ((), ())), preferred_element_type=jnp.float32
        )

    def run(step):
        head, _, rest = step.partition(":")
        if step == "ypre":
            send_pre(0, 2, "y")
        elif step == "cpre":
            send_pre(0, 1, "c")
        elif step == "rpre":
            waits["pre", 2].wait_recv()
            send_pre(2, 3, "c")
        elif step == "ccols":
            for r in (3, 2, 1, 0):
                for far in (1, 0):
                    send_columns("c", 1, "c", r, far, 0, 1)
        elif step == "cw":
            for b in range(blocks):
                rows = pl.ds(b * block_rows, block_rows)
                waits["own", b] = send(
                    weights.at[0, rows, :],
                    weights.at[1, rows, :],
                    own_send.at[b],
                    own_recv.at[b],
                    "c",
                )
        elif head[:2] == "yc":
            r, far = int(head[2]), head[3] == "f"
            send_columns("y", 2, "y", r, int(far), 1, 0)
            send_columns("d", 3, "d", r, int(far), 1, 1)
        elif head[:2] == "xw":
            group, key = int(head[2:]), (int(rest[0]), int(rest[1]))
            send_unit(0, 2, group, key, key, "x")
        elif head[0] == "o":
            use(0, int(head[1]) * block_rows, block_rows)
        elif head[0] == "p":
            waits["own", int(head[1])].wait_recv()
            use(1, int(head[1]) * block_rows, block_rows)
        elif head[0] == "w":
            group, key = int(head[1:]), (int(rest[0]), int(rest[1]))
            waits["w", 2, group, key].wait_recv()
            for peer, there in ROUTES[GROUPS[group]][key][1].items():
                send_unit(2, 2, group, key, there, peer)
            send_unit(2, 3, group, key, key, "c")
        elif head[0] in "uv":
            group, key = int(head[1:]), (int(rest[0]), int(rest[1]))
            slot = 2 if head[0] == "u" else 3
            if slot == 3:
                waits["w", 3, group, key].wait_recv()
            use(slot, unit_first(group, key), unit_rows)
        elif head[0] == "g":
            r, far = int(head[1]), head[2] == "f"
            if step == "g3f":
                waits["pre", 1].wait_recv()
                waits["pre", 3].wait_recv()
            if far:
                out_x[r] = piece(r, 1).astype(jnp.bfloat16)
                waits["x", r] = send(
                    out_x.at[r], in_x.at[r], sum_send.at[r], sum_recv.at[r], "x"
                )
            else:
                kept[r] = piece(r, 0)
        elif head[0] == "s":
            r = int(head[1])
            waits["x", r].wait_recv()
            value = kept[r] + in_x[r].astype(jnp.float32)
            if r == 2:
                waits["z", 3].wait_recv()
                value = value + in_z[1].astype(jnp.float32)
            slot = {1: 0, 3: 1, 2: 2}[r]
            out_z[slot] = value.astype(jnp.bfloat16)
            waits["z", r] = send(
                out_z.at[slot],
                in_z.at[slot],
                sum_send.at[DEPTH + slot],
                sum_recv.at[DEPTH + slot],
                "f" if r == 2 else "z",
            )
        elif step == "fin":
            keys_ref[...] = turn(projected[...], cosine, signed_sine).astype(jnp.bfloat16)
            waits["x", 0].wait_recv()
            summed = kept[0] + in_x[0].astype(jnp.float32)
            for r, slot in ((1, 0), (2, 2)):
                waits["z", r].wait_recv()
                summed = summed + in_z[slot].astype(jnp.float32)
            weight_grad_ref[...] = summed * (1.0 / math.sqrt(total))
        elif step == "bar":
            pl.semaphore_wait(barrier, len(peers))
        else:
            raise ValueError(step)

    steps = ORDER
    if "bar" not in steps:
        run("bar")
    for step in steps:
        run(step)
    for copy in sends:
        copy.wait_send()


def fused(tokens, key_codes, key_exponents, key_cotangent):
    nodes = lax.axis_size("node")
    locals_ = lax.axis_size("local")
    count, width = tokens.shape
    shard_rows, features = key_codes.shape
    row_count = width // (nodes * locals_)
    units = sum(SIZES[g] for g in GROUPS)
    half = THETA ** (-(np.arange(HEAD // 2) * 2.0 / HEAD))
    inverse = jnp.asarray(np.concatenate([half, half])[None, :], jnp.float32)
    anywhere = pl.BlockSpec(memory_space=pl.ANY)
    vmem = pl.BlockSpec(memory_space=pltpu.VMEM)
    dma = pltpu.SemaphoreType.DMA
    return pl.pallas_call(
        fused_kernel,
        out_shape=(
            pltpu.VMEM((count, features), jnp.bfloat16),
            pltpu.VMEM((count, width), jnp.bfloat16),
            pltpu.VMEM((row_count, features), jnp.float32),
        ),
        in_specs=[anywhere, anywhere, vmem, vmem, vmem],
        out_specs=(vmem, vmem, vmem),
        scratch_shapes=[
            pltpu.VMEM((count, width), jnp.bfloat16),
            pltpu.VMEM((shard_rows, features), jnp.bfloat16),
            pltpu.VMEM((2 * DEPTH, locals_ * count, row_count), jnp.bfloat16),
            pltpu.VMEM((locals_ * count, features), jnp.bfloat16),
            pltpu.VMEM((locals_, shard_rows, features), jnp.bfloat16),
            pltpu.VMEM((DEPTH, row_count, features), jnp.bfloat16),
            pltpu.VMEM((DEPTH, row_count, features), jnp.bfloat16),
            pltpu.VMEM((DEPTH - 1, row_count, features), jnp.bfloat16),
            pltpu.VMEM((DEPTH - 1, row_count, features), jnp.bfloat16),
            pltpu.VMEM((DEPTH, row_count, features), jnp.float32),
            pltpu.VMEM((count, features), jnp.float32),
            dma((2,)),
            dma((2 * DEPTH,)),
            dma((2 * DEPTH, 4)),
            dma((2 * DEPTH, 4)),
            dma((4,)),
            dma((4,)),
            dma((4,)),
            dma((4,)),
            dma((4, units)),
            dma((2, units)),
            dma((2 * DEPTH,)),
            dma((2 * DEPTH,)),
        ],
        compiler_params=pltpu.CompilerParams(collective_id=0, has_side_effects=True),
    )(tokens, key_codes, key_exponents.T, key_cotangent, inverse)


def solution(mesh):
    def body(tokens, key_codes, key_exponents, key_cotangent):
        nodes, locals_ = mesh.shape["node"], mesh.shape["local"]
        row_count = tokens.shape[1] // (nodes * locals_)
        grid = nodes == 2 * DEPTH and locals_ == 2 * CORES
        run = fused if grid and row_count % HEAD == 0 else on_device
        return run(tokens, key_codes, key_exponents, key_cotangent)

    return jax.shard_map(
        body,
        mesh=mesh,
        in_specs=(
            P(("node", "local"), None),
            P("local", None),
            P("local", None),
            P(("node", "local"), None),
        ),
        out_specs=(
            P(("node", "local"), None),
            P(("node", "local"), None),
            P(("node", "local"), None),
        ),
        check_vma=False,
    )
```

time: 45.1 us -> 39.5 us (0.88)
  Pallas kernels: 41.9 us -> 36.4 us
    pallas_call x1, Pallas kernels: 41.9 us -> 36.4 us  [fused(): pl.pallas_call(fused_kernel, out_shape=(pltpu.VMEM((count, features), jnp...]
where the time goes in v1:
time: 39.5 us; the launch traced here: 39.3 us
  Pallas kernels  36.4 us (92%)
  local copies, waits for them, and re-layouts  2.33 us (6%)
  between operations  0.64 us (2%)
    pallas_call x1, Pallas kernels, fused(): pl.pallas_call(fused_kernel, out_shape=(pltpu.VMEM((count, features), jnp...  36.4 us
    unnamed x3, local copies, waits for them, and re-layouts  2.33 us

profile of v1, /device:TPU:0, one launch (start us, length us, event | category | flops | bytes accessed | tf_op | source)
XLA Modules:
  0.0 39.3 jit_solution(311019288056731676)
XLA Ops:
  0.6 36.4 %shard_map.76 = (bf16[128,512]{1,0:T(8,128)(2,1)S(1)}, bf16[128,4096]{1,0:T(8,128)(2,1)S(1)}, f32[128,512]{1,0:T(8,128)S(1)}) custom-call(bf16[128,4096]{1,0:T(8,128)(2,1)} %tokens_hbm.1, bf16[1024,512]{1,0:T(8,128)(2,1)} %codes_hbm.1, s32[2,1024]{1,0:T(2,128)} %bitcast.1, bf16[128,512]{1,0:T(8,128)(2,1)} %cotangent_ref.1, f32[1,128]{1,0:T(1,128)} %constant.2.clone.inverse_ref), custom_call_target="tpu_custom_call" | custom-call | tf_op jit(solution)/shard_map/pallas_call | solution.py:480
  37.0 0.7 %copy.11 = bf16[128,512]{1,0:T(8,128)(2,1)} copy(bf16[128,512]{1,0:T(8,128)(2,1)S(1)} %get-tuple-element.3) | data formatting | bytes 262144
  37.7 0.7 %copy.13 = f32[128,512]{1,0:T(8,128)} copy(f32[128,512]{1,0:T(8,128)S(1)} %get-tuple-element.5) | data formatting | bytes 524288
  38.4 1.0 %copy.12 = bf16[128,4096]{1,0:T(8,128)(2,1)} copy(bf16[128,4096]{1,0:T(8,128)(2,1)S(1)} %get-tuple-element.4) | data formatting | bytes 2097152

commit v2 on v1

--- a/solution.py
+++ b/solution.py
@@ -135,7 +135,7 @@
 
 CORES = 2
 DEPTH = 4
-GROUPS = ("S1", "P2z", "P2z")
+GROUPS = ('S1', 'P2z', 'P2z')
 ROUTES = {
     "S1": {
         (0, 0): ("x", {"z": (1, 0), "y": (0, 1)}),
@@ -152,30 +152,19 @@
     "P2z": {(0, 0): ("x", {"z": (1, 0)}), (1, 0): ("z", {})},
     "P2y": {(0, 0): ("x", {"y": (0, 1)}), (0, 1): ("y", {})},
 }
+SPLIT = 2
+PARTS = 2
 SIZES = {"S1": 4, "S2": 4, "P2z": 2, "P2y": 2}
 ORDER = (
-    "xw0:00", "ypre", "cpre", "yc3f", "ccols", "cw", "yc2f", "yc3n", "xw1:00", "yc1f", "yc2n", "yc0f", "yc1n",
-    "o0", "o1", "o2", "o3",
-    "w0:00",
-    "rpre",
-    "p0", "p1",
-    "g3f", "xw2:00",
-    "w1:00", "p2",
-    "g2f", "p3",
-    "g3n", "u0:00", "v0:00",
-    "w0:10", "g1f", "g2n",
-    "u1:00", "v1:00",
-    "s3",
-    "g0f", "g1n",
-    "w1:10", "w2:00", "u0:10", "v0:10",
-    "u1:10", "v1:10", "u2:00", "v2:00",
-    "yc0n",
-    "w2:10",
-    "s2", "s1",
-    "u2:10", "v2:10",
-    "w0:01", "u0:01", "v0:01",
-    "w0:11", "g0n", "u0:11", "v0:11",
-    "fin",
+    "xw1:00", "ypre", "yc2n", "xw2:00", "ccols", "yc3f", "cw", "w1:00.0",
+    "yc2f", "p1", "yc3n", "yc1f", "p2", "xw0:00", "yc0f", "rpre",
+    "w1:00.1", "cpre", "w2:00.0", "yc1n", "w2:00.1", "g3f", "w0:00.0", "w1:10.1",
+    "g2f", "p0", "g2n", "w0:00.1", "w1:10.0", "g3n", "o3", "o1",
+    "s00", "g1f", "u0:00", "s01", "w0:10.1", "u1:00", "o2", "w0:10.0",
+    "s10", "v0:10", "g1n", "g0f", "s11", "w2:10.0", "s20", "s21",
+    "v0:00", "yc0n", "w0:11.1", "w0:01.1", "w0:01.0", "w2:10.1", "u2:10", "u2:00",
+    "o0", "u0:01", "w0:11.0", "u0:11", "u1:10", "v2:00", "v0:01", "v1:00",
+    "u0:10", "v0:11", "v1:10", "p3", "v2:10", "key", "g0n", "fin",
 )
 
 
@@ -211,6 +200,8 @@
     weight_recv,
     sum_send,
     sum_recv,
+    line_send,
+    line_recv,
 ):
     node = lax.axis_index("node")
     local = lax.axis_index("local")
@@ -219,20 +210,30 @@
     count = tokens.shape[0]
     row_count = columns.shape[2]
     shard_rows = weights.shape[1]
+    features = pre.shape[1]
     unit_rows = shard_rows // sum(SIZES[g] for g in GROUPS)
+    part_rows = unit_rows // PARTS
+    width = features // SPLIT
     total = count * nodes * locals_
 
+    depth_at = lax.div(node, 2)
+    inner = lax.div(depth_at * (DEPTH - 1 - depth_at), 2)
     peers = {
         "c": (node, flip(local, 1)),
         "x": (node, flip(local, 2)),
         "y": (flip(node, 1), local),
         "d": (flip(node, 1), flip(local, 1)),
         "z": (flip(node, 2), local),
-        "f": (flip(node, 4), local),
     }
+    neighbours = len(peers)
     barrier = pltpu.get_barrier_semaphore()
     for peer in peers.values():
         pl.semaphore_signal(barrier, inc=1, device_id=peer, device_id_type=MESH)
+    peers["m"] = (flip(node, 6), local)
+
+    @pl.when(inner == 1)
+    def _():
+        pl.semaphore_signal(barrier, inc=1, device_id=peers["m"], device_id_type=MESH)
 
     load_codes = pltpu.make_async_copy(codes_hbm, codes, load_sem.at[0])
     load_codes.start()
@@ -245,6 +246,9 @@
 
     def slot_rows(slot):
         return pl.ds(slot * count, count)
+
+    def lanes_of(k):
+        return pl.ds(k * width, width)
 
     own = {}
     for r in range(DEPTH):
@@ -278,9 +282,10 @@
     projected[...] = jnp.zeros_like(projected)
 
     sends = []
-
-    def send(src, dst, send_sem, recv_sem, peer):
-        copy = pltpu.make_async_remote_copy(
+    waits = {}
+
+    def describe(src, dst, send_sem, recv_sem, peer):
+        return pltpu.make_async_remote_copy(
             src_ref=src,
             dst_ref=dst,
             send_sem=send_sem,
@@ -288,11 +293,12 @@
             device_id=peers[peer],
             device_id_type=MESH,
         )
+
+    def send(src, dst, send_sem, recv_sem, peer):
+        copy = describe(src, dst, send_sem, recv_sem, peer)
         copy.start()
         sends.append(copy)
         return copy
-
-    waits = {}
 
     def send_columns(name, slot, peer, r, far, e, d):
         k = 2 * r + far
@@ -331,7 +337,7 @@
             tokens[:, lanes], block, preferred_element_type=jnp.float32
         )
 
-    zbit = lax.rem(lax.div(node, 2), 2)
+    zbit = lax.rem(depth_at, 2)
     ybit = lax.rem(node, 2)
     bases = [sum(SIZES[g] for g in GROUPS[:i]) for i in range(len(GROUPS))]
 
@@ -348,14 +354,15 @@
         dz, dy = key
         return bases[group] + {"S1": 2 * dz + dy, "S2": 2 * dz + dy, "P2z": dz, "P2y": dy}[kind]
 
-    def send_unit(source, slot, group, source_key, key, peer):
-        rows = pl.ds(unit_first(group, source_key), unit_rows)
+    def send_unit(source, slot, group, source_key, key, part, peer):
+        first = unit_first(group, source_key) + part * part_rows
+        rows = pl.ds(pl.multiple_of(first, part_rows), part_rows)
         lane_of = {"x": 0, "y": 1, "z": 2, "c": 3}[peer]
-        waits["w", slot, group, key] = send(
+        waits["w", slot, group, key, part] = send(
             weights.at[source, rows, :],
             weights.at[slot, rows, :],
-            weight_send.at[lane_of, sem_index(group, source_key)],
-            weight_recv.at[slot - 2, sem_index(group, key)],
+            weight_send.at[lane_of, sem_index(group, source_key), part],
+            weight_recv.at[slot - 2, sem_index(group, key), part],
             peer,
         )
 
@@ -367,6 +374,52 @@
         return lax.dot_general(
             columns[k], pre[...], (((0,), (0,)), ((), ())), preferred_element_type=jnp.float32
         )
+
+    line = {}
+    for i in range(DEPTH - 1):
+        for k in range(SPLIT):
+            for middle in range(2):
+                slot = i + DEPTH - 1 if middle and i < 2 else i
+                line[middle, i, k] = describe(
+                    out_z.at[i * SPLIT + k],
+                    in_z.at[slot * SPLIT + k],
+                    line_send.at[i * SPLIT + k],
+                    line_recv.at[slot * SPLIT + k],
+                    "m" if middle and i < 2 else "z",
+                )
+    order_of = ((3, 2, 1), (2, 3, 1))
+
+    def chain(i, k):
+        for middle in range(2):
+
+            @pl.when(inner == middle)
+            def _():
+                r = order_of[middle][i]
+                waits["x", r, k].wait_recv()
+                value = kept[r, :, lanes_of(k)] + in_x[r * SPLIT + k].astype(jnp.float32)
+                if middle:
+                    line[0 if i < 2 else 1, i if i < 2 else 0, k].wait_recv()
+                    slot = i if i < 2 else DEPTH - 1
+                    value = value + in_z[slot * SPLIT + k].astype(jnp.float32)
+                out_z[i * SPLIT + k] = value.astype(jnp.bfloat16)
+                line[middle, i, k].start()
+
+    gain = 1.0 / math.sqrt(total)
+
+    def finish(k):
+        waits["x", 0, k].wait_recv()
+        summed = kept[0, :, lanes_of(k)] + in_x[k].astype(jnp.float32)
+        line[0, 2, k].wait_recv()
+        summed = summed + in_z[2 * SPLIT + k].astype(jnp.float32)
+        weight_grad_ref[:, lanes_of(k)] = summed * gain
+
+        @pl.when(inner == 1)
+        def _():
+            line[1, 1, k].wait_recv()
+            last = in_z[DEPTH * SPLIT + k].astype(jnp.float32)
+            weight_grad_ref[:, lanes_of(k)] += last * gain
+
+    pre_ready = []
 
     def run(step):
         head, _, rest = step.partition(":")
@@ -392,12 +445,13 @@
                     "c",
                 )
         elif head[:2] == "yc":
-            r, far = int(head[2]), head[3] == "f"
-            send_columns("y", 2, "y", r, int(far), 1, 0)
-            send_columns("d", 3, "d", r, int(far), 1, 1)
+            r, far = int(head[2]), int(head[3] == "f")
+            send_columns("y", 2, "y", r, far, 1, 0)
+            send_columns("d", 3, "d", r, far, 1, 1)
         elif head[:2] == "xw":
             group, key = int(head[2:]), (int(rest[0]), int(rest[1]))
-            send_unit(0, 2, group, key, key, "x")
+            for part in range(PARTS):
+                send_unit(0, 2, group, key, key, part, "x")
         elif head[0] == "o":
             use(0, int(head[1]) * block_rows, block_rows)
         elif head[0] == "p":
@@ -405,54 +459,43 @@
             use(1, int(head[1]) * block_rows, block_rows)
         elif head[0] == "w":
             group, key = int(head[1:]), (int(rest[0]), int(rest[1]))
-            waits["w", 2, group, key].wait_recv()
+            part = int(rest[3])
+            waits["w", 2, group, key, part].wait_recv()
             for peer, there in ROUTES[GROUPS[group]][key][1].items():
-                send_unit(2, 2, group, key, there, peer)
-            send_unit(2, 3, group, key, key, "c")
+                send_unit(2, 2, group, key, there, part, peer)
+            send_unit(2, 3, group, key, key, part, "c")
         elif head[0] in "uv":
             group, key = int(head[1:]), (int(rest[0]), int(rest[1]))
             slot = 2 if head[0] == "u" else 3
             if slot == 3:
-                waits["w", 3, group, key].wait_recv()
+                for part in range(PARTS):
+                    waits["w", 3, group, key, part].wait_recv()
             use(slot, unit_first(group, key), unit_rows)
         elif head[0] == "g":
-            r, far = int(head[1]), head[2] == "f"
-            if step == "g3f":
+            r, far = int(head[1]), int(head[2] == "f")
+            if not pre_ready:
                 waits["pre", 1].wait_recv()
                 waits["pre", 3].wait_recv()
+                pre_ready.append(True)
+            value = piece(r, far)
             if far:
-                out_x[r] = piece(r, 1).astype(jnp.bfloat16)
-                waits["x", r] = send(
-                    out_x.at[r], in_x.at[r], sum_send.at[r], sum_recv.at[r], "x"
-                )
+                for k in range(SPLIT):
+                    at = r * SPLIT + k
+                    out_x[at] = value[:, k * width : (k + 1) * width].astype(jnp.bfloat16)
+                    waits["x", r, k] = send(
+                        out_x.at[at], in_x.at[at], sum_send.at[at], sum_recv.at[at], "x"
+                    )
             else:
-                kept[r] = piece(r, 0)
+                kept[r] = value
         elif head[0] == "s":
-            r = int(head[1])
-            waits["x", r].wait_recv()
-            value = kept[r] + in_x[r].astype(jnp.float32)
-            if r == 2:
-                waits["z", 3].wait_recv()
-                value = value + in_z[1].astype(jnp.float32)
-            slot = {1: 0, 3: 1, 2: 2}[r]
-            out_z[slot] = value.astype(jnp.bfloat16)
-            waits["z", r] = send(
-                out_z.at[slot],
-                in_z.at[slot],
-                sum_send.at[DEPTH + slot],
-                sum_recv.at[DEPTH + slot],
-                "f" if r == 2 else "z",
-            )
+            chain(int(head[1]), int(head[2]))
+        elif step == "key":
+            keys_ref[...] = turn(projected[...], cosine, signed_sine).astype(jnp.bfloat16)
         elif step == "fin":
-            keys_ref[...] = turn(projected[...], cosine, signed_sine).astype(jnp.bfloat16)
-            waits["x", 0].wait_recv()
-            summed = kept[0] + in_x[0].astype(jnp.float32)
-            for r, slot in ((1, 0), (2, 2)):
-                waits["z", r].wait_recv()
-                summed = summed + in_z[slot].astype(jnp.float32)
-            weight_grad_ref[...] = summed * (1.0 / math.sqrt(total))
+            for k in range(SPLIT):
+                finish(k)
         elif step == "bar":
-            pl.semaphore_wait(barrier, len(peers))
+            pl.semaphore_wait(barrier, neighbours + inner)
         else:
             raise ValueError(step)
 
@@ -463,6 +506,13 @@
         run(step)
     for copy in sends:
         copy.wait_send()
+    for middle in range(2):
+
+        @pl.when(inner == middle)
+        def _():
+            for i in range(DEPTH - 1):
+                for k in range(SPLIT):
+                    line[middle, i, k].wait_send()
 
 
 def fused(tokens, key_codes, key_exponents, key_cotangent):
@@ -492,10 +542,10 @@
             pltpu.VMEM((2 * DEPTH, locals_ * count, row_count), jnp.bfloat16),
             pltpu.VMEM((locals_ * count, features), jnp.bfloat16),
             pltpu.VMEM((locals_, shard_rows, features), jnp.bfloat16),
-            pltpu.VMEM((DEPTH, row_count, features), jnp.bfloat16),
-            pltpu.VMEM((DEPTH, row_count, features), jnp.bfloat16),
-            pltpu.VMEM((DEPTH - 1, row_count, features), jnp.bfloat16),
-            pltpu.VMEM((DEPTH - 1, row_count, features), jnp.bfloat16),
+            pltpu.VMEM((DEPTH * SPLIT, row_count, features // SPLIT), jnp.bfloat16),
+            pltpu.VMEM((DEPTH * SPLIT, row_count, features // SPLIT), jnp.bfloat16),
+            pltpu.VMEM((3 * SPLIT, row_count, features // SPLIT), jnp.bfloat16),
+            pltpu.VMEM((5 * SPLIT, row_count, features // SPLIT), jnp.bfloat16),
             pltpu.VMEM((DEPTH, row_count, features), jnp.float32),
             pltpu.VMEM((count, features), jnp.float32),
             dma((2,)),
@@ -506,10 +556,12 @@
             dma((4,)),
             dma((4,)),
             dma((4,)),
-            dma((4, units)),
-            dma((2, units)),
-            dma((2 * DEPTH,)),
-            dma((2 * DEPTH,)),
+            dma((4, units, PARTS)),
+            dma((2, units, PARTS)),
+            dma((DEPTH * SPLIT,)),
+            dma((DEPTH * SPLIT,)),
+            dma((3 * SPLIT,)),
+            dma((5 * SPLIT,)),
         ],
         compiler_params=pltpu.CompilerParams(collective_id=0, has_side_effects=True),
     )(tokens, key_codes, key_exponents.T, key_cotangent, inverse)

time: 39.5 us -> 35.4 us (0.90)
  Pallas kernels: 36.4 us -> 32.3 us
    pallas_call x1, Pallas kernels: 36.4 us -> 32.3 us  [fused(): pl.pallas_call(fused_kernel, out_shape=(pltpu.VMEM((count, features), jnp...]
where the time goes in v2:
time: 35.4 us; the launch traced here: 35.3 us
  Pallas kernels  32.3 us (91%)
  local copies, waits for them, and re-layouts  2.33 us (7%)
  between operations  0.64 us (2%)
    pallas_call x1, Pallas kernels, fused(): pl.pallas_call(fused_kernel, out_shape=(pltpu.VMEM((count, features), jnp...  32.3 us
    unnamed x3, local copies, waits for them, and re-layouts  2.33 us

profile of v2, /device:TPU:0, one launch (start us, length us, event | category | flops | bytes accessed | tf_op | source)
XLA Modules:
  0.0 35.3 jit_solution(11995258206435423740)
XLA Ops:
  0.6 32.3 %shard_map.76 = (bf16[128,512]{1,0:T(8,128)(2,1)S(1)}, bf16[128,4096]{1,0:T(8,128)(2,1)S(1)}, f32[128,512]{1,0:T(8,128)S(1)}) custom-call(bf16[128,4096]{1,0:T(8,128)(2,1)} %tokens_hbm.1, bf16[1024,512]{1,0:T(8,128)(2,1)} %codes_hbm.1, s32[2,1024]{1,0:T(2,128)} %bitcast.1, bf16[128,512]{1,0:T(8,128)(2,1)} %cotangent_ref.1, f32[1,128]{1,0:T(1,128)} %constant.2.clone.inverse_ref), custom_call_target="tpu_custom_call" | custom-call | tf_op jit(solution)/shard_map/pallas_call | solution.py:530
  33.0 0.7 %copy.11 = bf16[128,512]{1,0:T(8,128)(2,1)} copy(bf16[128,512]{1,0:T(8,128)(2,1)S(1)} %get-tuple-element.3) | data formatting | bytes 262144
  33.6 0.7 %copy.13 = f32[128,512]{1,0:T(8,128)} copy(f32[128,512]{1,0:T(8,128)S(1)} %get-tuple-element.5) | data formatting | bytes 524288
  34.3 1.0 %copy.12 = bf16[128,4096]{1,0:T(8,128)(2,1)} copy(bf16[128,4096]{1,0:T(8,128)(2,1)S(1)} %get-tuple-element.4) | data formatting | bytes 2097152

commit v3 on v2

--- a/solution.py
+++ b/solution.py
@@ -156,29 +156,35 @@
 PARTS = 2
 SIZES = {"S1": 4, "S2": 4, "P2z": 2, "P2y": 2}
 ORDER = (
-    "xw1:00", "ypre", "yc2n", "xw2:00", "ccols", "yc3f", "cw", "w1:00.0",
-    "yc2f", "p1", "yc3n", "yc1f", "p2", "xw0:00", "yc0f", "rpre",
-    "w1:00.1", "cpre", "w2:00.0", "yc1n", "w2:00.1", "g3f", "w0:00.0", "w1:10.1",
-    "g2f", "p0", "g2n", "w0:00.1", "w1:10.0", "g3n", "o3", "o1",
-    "s00", "g1f", "u0:00", "s01", "w0:10.1", "u1:00", "o2", "w0:10.0",
-    "s10", "v0:10", "g1n", "g0f", "s11", "w2:10.0", "s20", "s21",
-    "v0:00", "yc0n", "w0:11.1", "w0:01.1", "w0:01.0", "w2:10.1", "u2:10", "u2:00",
-    "o0", "u0:01", "w0:11.0", "u0:11", "u1:10", "v2:00", "v0:01", "v1:00",
-    "u0:10", "v0:11", "v1:10", "p3", "v2:10", "key", "g0n", "fin",
+    "exp", "bar", "xw1:00", "yc3f", "xw0:00", "deq", "trg", "ypre",
+    "cw", "yc2n", "yc3n", "xw2:00", "w1:00.0", "ccols", "yc2f", "yc1f",
+    "cpre", "o3", "o0", "yc1n", "w1:00.1", "yc0f", "w0:00.0", "rpre",
+    "w0:00.1", "g3f", "g2n", "w2:00.0", "v0:00", "u1:00", "v1:00", "w1:10.0",
+    "w0:10.0", "w2:00.1", "g2f", "g3n", "u0:00", "s00", "g1f", "w0:10.1",
+    "p0", "s01", "o2", "u2:00", "v0:10", "w2:10.1", "p1", "s10",
+    "yc0n", "g0f", "p2", "g1n", "w1:10.1", "s11", "s20", "w0:01.1",
+    "w2:10.0", "u2:10", "w0:01.0", "u0:10", "v1:10", "u0:01", "s21", "u1:10",
+    "w0:11.1", "v2:10", "w0:11.0", "p3", "g0n", "o1", "v0:11", "v0:01",
+    "u0:11", "v2:00", "key", "fin",
 )
 
 
 def fused_kernel(
     tokens_hbm,
     codes_hbm,
-    exponents_ref,
-    cotangent_ref,
-    inverse_ref,
+    exponents_hbm,
+    cotangent_hbm,
+    inverse_hbm,
     keys_ref,
     input_grad_ref,
     weight_grad_ref,
     tokens,
     codes,
+    exponents_ref,
+    cotangent_ref,
+    inverse_ref,
+    scale_ref,
+    rotation,
     columns,
     pre,
     weights,
@@ -235,11 +241,6 @@
     def _():
         pl.semaphore_signal(barrier, inc=1, device_id=peers["m"], device_id_type=MESH)
 
-    load_codes = pltpu.make_async_copy(codes_hbm, codes, load_sem.at[0])
-    load_codes.start()
-    load_tokens = pltpu.make_async_copy(tokens_hbm, tokens, load_sem.at[1])
-    load_tokens.start()
-
     def owned(r, far, e=0, d=0):
         first = (flip(node, 2 * r + e) * locals_ + flip(local, 2 * far + d)) * row_count
         return pl.ds(pl.multiple_of(first, row_count), row_count)
@@ -250,36 +251,84 @@
     def lanes_of(k):
         return pl.ds(k * width, width)
 
+    zbit = lax.rem(depth_at, 2)
+    ybit = lax.rem(node, 2)
+    bases = [sum(SIZES[g] for g in GROUPS[:i]) for i in range(len(GROUPS))]
+
+    def unit_first(group, key):
+        kind = GROUPS[group]
+        dz, dy = key
+        zz = 1 - zbit if dz else zbit
+        yy = 1 - ybit if dy else ybit
+        index = {"S1": 2 * zz + yy, "S2": 2 * zz + yy, "P2z": zz, "P2y": yy}[kind]
+        return pl.multiple_of((bases[group] + index) * unit_rows, unit_rows)
+
+    def sem_index(group, key):
+        kind = GROUPS[group]
+        dz, dy = key
+        return bases[group] + {"S1": 2 * dz + dy, "S2": 2 * dz + dy, "P2z": dz, "P2y": dy}[kind]
+
+    def load(source, target, at):
+        copy = pltpu.make_async_copy(source, target, load_sem.at[at])
+        copy.start()
+        return copy
+
+    load_exponents = load(exponents_hbm, exponents_ref, 0)
+    load_codes = {}
+    keys = [(g, key) for g in range(len(GROUPS)) for key in ROUTES[GROUPS[g]]]
+    first_keys = [(g, key) for g, key in keys if ROUTES[GROUPS[g]][key][0] == "x"]
+    rest_keys = [pair for pair in keys if pair not in first_keys]
+
+    def start_codes(pairs):
+        for g, key in pairs:
+            rows = pl.ds(unit_first(g, key), unit_rows)
+            load_codes[g, key] = load(
+                codes_hbm.at[rows, :], codes.at[rows, :], 4 + sem_index(g, key)
+            )
+
+    start_codes(first_keys)
+    load_inverse = load(inverse_hbm, inverse_ref, 1)
+    load_cotangent = load(cotangent_hbm, cotangent_ref, 2)
+    start_codes(rest_keys)
+    load_tokens = load(tokens_hbm, tokens, 3)
     own = {}
-    for r in range(DEPTH):
-        for far in range(2):
+    for r in range(DEPTH - 1, -1, -1):
+        for far in range(1, -1, -1):
             k = 2 * r + far
             own[k] = pltpu.make_async_copy(
                 tokens_hbm.at[:, owned(r, far)], columns.at[k, slot_rows(0), :], own_sem.at[k]
             )
             own[k].start()
 
-    start = lax.rem((node * locals_ + local) * count, SEQ)
-    positions = lax.rem(start + lax.broadcasted_iota(jnp.int32, (count, HEAD), 0), SEQ)
-    angles = positions.astype(jnp.float32) * inverse_ref[...]
-    cosine = jnp.cos(angles)
-    sine = jnp.sin(angles)
-    lane = lax.broadcasted_iota(jnp.int32, (count, HEAD), 1)
-    signed_sine = jnp.where(lane < HEAD // 2, -sine, sine)
-    pre[slot_rows(0), :] = turn(
-        cotangent_ref[...].astype(jnp.float32), cosine, -signed_sine
-    ).astype(jnp.bfloat16)
-
-    load_codes.wait()
-    scale = jnp.left_shift(1, exponents_ref[...] + 15).astype(jnp.float32) * (2.0**-15)
-    scale = jnp.transpose(jnp.concatenate([scale] * (8 // scale.shape[0]), axis=0))
-    for block in range(codes.shape[1] // QBLOCK):
-        lanes = pl.ds(block * QBLOCK, QBLOCK)
-        weights[0, :, lanes] = (
-            codes[:, lanes].astype(jnp.float32) * scale[:, block : block + 1]
+    def rotations():
+        start = lax.rem((node * locals_ + local) * count, SEQ)
+        positions = lax.rem(start + lax.broadcasted_iota(jnp.int32, (count, HEAD), 0), SEQ)
+        load_inverse.wait()
+        angles = positions.astype(jnp.float32) * inverse_ref[...]
+        cosine = jnp.cos(angles)
+        sine = jnp.sin(angles)
+        lane = lax.broadcasted_iota(jnp.int32, (count, HEAD), 1)
+        signed_sine = jnp.where(lane < HEAD // 2, -sine, sine)
+        rotation[0] = cosine
+        rotation[1] = signed_sine
+        load_cotangent.wait()
+        pre[slot_rows(0), :] = turn(
+            cotangent_ref[...].astype(jnp.float32), cosine, -signed_sine
         ).astype(jnp.bfloat16)
-    load_tokens.wait()
-    projected[...] = jnp.zeros_like(projected)
+
+    def scales():
+        load_exponents.wait()
+        scale = jnp.left_shift(1, exponents_ref[...] + 15).astype(jnp.float32) * (2.0**-15)
+        scale_ref[...] = jnp.transpose(jnp.concatenate([scale] * (8 // scale.shape[0]), axis=0))
+
+    def expand(group, key):
+        load_codes[group, key].wait()
+        rows = pl.ds(unit_first(group, key), unit_rows)
+        for block in range(features // QBLOCK):
+            lanes = pl.ds(block * QBLOCK, QBLOCK)
+            weights[0, rows, lanes] = (
+                codes[rows, lanes].astype(jnp.float32) * scale_ref[rows, block : block + 1]
+            ).astype(jnp.bfloat16)
 
     sends = []
     waits = {}
@@ -303,7 +352,7 @@
     def send_columns(name, slot, peer, r, far, e, d):
         k = 2 * r + far
         waits[name, k] = send(
-            tokens.at[:, owned(r, far, e, d)],
+            tokens_hbm.at[:, owned(r, far, e, d)],
             columns.at[k, slot_rows(slot), :],
             column_send.at[k, slot],
             column_recv.at[k, slot],
@@ -337,23 +386,6 @@
             tokens[:, lanes], block, preferred_element_type=jnp.float32
         )
 
-    zbit = lax.rem(depth_at, 2)
-    ybit = lax.rem(node, 2)
-    bases = [sum(SIZES[g] for g in GROUPS[:i]) for i in range(len(GROUPS))]
-
-    def unit_first(group, key):
-        kind = GROUPS[group]
-        dz, dy = key
-        zz = 1 - zbit if dz else zbit
-        yy = 1 - ybit if dy else ybit
-        index = {"S1": 2 * zz + yy, "S2": 2 * zz + yy, "P2z": zz, "P2y": yy}[kind]
-        return pl.multiple_of((bases[group] + index) * unit_rows, unit_rows)
-
-    def sem_index(group, key):
-        kind = GROUPS[group]
-        dz, dy = key
-        return bases[group] + {"S1": 2 * dz + dy, "S2": 2 * dz + dy, "P2z": dz, "P2y": dy}[kind]
-
     def send_unit(source, slot, group, source_key, key, part, peer):
         first = unit_first(group, source_key) + part * part_rows
         rows = pl.ds(pl.multiple_of(first, part_rows), part_rows)
@@ -427,6 +459,17 @@
             send_pre(0, 2, "y")
         elif step == "cpre":
             send_pre(0, 1, "c")
+        elif step == "exp":
+            scales()
+            for group, key in first_keys:
+                expand(group, key)
+        elif step == "trg":
+            rotations()
+        elif step == "deq":
+            for group, key in rest_keys:
+                expand(group, key)
+            load_tokens.wait()
+            projected[...] = jnp.zeros_like(projected)
         elif step == "rpre":
             waits["pre", 2].wait_recv()
             send_pre(2, 3, "c")
@@ -490,7 +533,7 @@
         elif head[0] == "s":
             chain(int(head[1]), int(head[2]))
         elif step == "key":
-            keys_ref[...] = turn(projected[...], cosine, signed_sine).astype(jnp.bfloat16)
+            keys_ref[...] = turn(projected[...], rotation[0], rotation[1]).astype(jnp.bfloat16)
         elif step == "fin":
             for k in range(SPLIT):
                 finish(k)
@@ -513,6 +556,14 @@
             for i in range(DEPTH - 1):
                 for k in range(SPLIT):
                     line[middle, i, k].wait_send()
+
+
+def place(*refs):
+    copies = [pltpu.make_async_copy(refs[i], refs[3 + i], refs[6].at[i]) for i in range(3)]
+    for copy in copies:
+        copy.start()
+    for copy in copies:
+        copy.wait()
 
 
 def fused(tokens, key_codes, key_exponents, key_cotangent):
@@ -527,18 +578,23 @@
     anywhere = pl.BlockSpec(memory_space=pl.ANY)
     vmem = pl.BlockSpec(memory_space=pltpu.VMEM)
     dma = pltpu.SemaphoreType.DMA
-    return pl.pallas_call(
+    held = pl.pallas_call(
         fused_kernel,
         out_shape=(
             pltpu.VMEM((count, features), jnp.bfloat16),
             pltpu.VMEM((count, width), jnp.bfloat16),
             pltpu.VMEM((row_count, features), jnp.float32),
         ),
-        in_specs=[anywhere, anywhere, vmem, vmem, vmem],
+        in_specs=[anywhere] * 5,
         out_specs=(vmem, vmem, vmem),
         scratch_shapes=[
             pltpu.VMEM((count, width), jnp.bfloat16),
             pltpu.VMEM((shard_rows, features), jnp.bfloat16),
+            pltpu.VMEM(key_exponents.shape[::-1], jnp.int32),
+            pltpu.VMEM((count, features), jnp.bfloat16),
+            pltpu.VMEM((1, HEAD), jnp.float32),
+            pltpu.VMEM((shard_rows, 8), jnp.float32),
+            pltpu.VMEM((2, count, HEAD), jnp.float32),
             pltpu.VMEM((2 * DEPTH, locals_ * count, row_count), jnp.bfloat16),
             pltpu.VMEM((locals_ * count, features), jnp.bfloat16),
             pltpu.VMEM((locals_, shard_rows, features), jnp.bfloat16),
@@ -548,7 +604,7 @@
             pltpu.VMEM((5 * SPLIT, row_count, features // SPLIT), jnp.bfloat16),
             pltpu.VMEM((DEPTH, row_count, features), jnp.float32),
             pltpu.VMEM((count, features), jnp.float32),
-            dma((2,)),
+            dma((4 + units,)),
             dma((2 * DEPTH,)),
             dma((2 * DEPTH, 4)),
             dma((2 * DEPTH, 4)),
@@ -565,6 +621,13 @@
         ],
         compiler_params=pltpu.CompilerParams(collective_id=0, has_side_effects=True),
     )(tokens, key_codes, key_exponents.T, key_cotangent, inverse)
+    return pl.pallas_call(
+        place,
+        out_shape=tuple(jax.ShapeDtypeStruct(a.shape, a.dtype) for a in held),
+        in_specs=[vmem] * 3,
+        out_specs=(anywhere,) * 3,
+        scratch_shapes=[dma((3,))],
+    )(*(pltpu.with_memory_space_constraint(a, pltpu.VMEM) for a in held))
 
 
 def solution(mesh):

time: 35.4 us -> 33.4 us (0.944)
  local copies, waits for them, and re-layouts: 2.33 us -> 0 us
    unnamed x3 -> x0, local copies, waits for them, and re-layouts: 2.33 us -> none
    pallas_call x0 -> x1, Pallas kernels: none -> 1.12 us  [fused(): pl.pallas_call(place, out_shape=tuple((jax.ShapeDtypeStruct(a.shape, a.dt...]
    pallas_call x1, Pallas kernels: 32.3 us -> 31.4 us  [fused(): pl.pallas_call(fused_kernel, out_shape=(pltpu.VMEM((count, features), jnp...]
where the time goes in v3:
time: 33.4 us; the launch traced here: 33.2 us
  Pallas kernels  32.5 us (97%)
  between operations  0.64 us (2%)
    pallas_call x1, Pallas kernels, fused(): pl.pallas_call(fused_kernel, out_shape=(pltpu.VMEM((count, features), jnp...  31.4 us
    pallas_call x1, Pallas kernels, fused(): pl.pallas_call(place, out_shape=tuple((jax.ShapeDtypeStruct(a.shape, a.dt...  1.12 us

profile of v3, /device:TPU:0, one launch (start us, length us, event | category | flops | bytes accessed | tf_op | source)
XLA Modules:
  0.0 33.2 jit_solution(13817289451306310000)
XLA Ops:
  0.6 31.4 %shard_map.76 = (bf16[128,512]{1,0:T(8,128)(2,1)S(1)}, bf16[128,4096]{1,0:T(8,128)(2,1)S(1)}, f32[128,512]{1,0:T(8,128)S(1)}) custom-call(bf16[128,4096]{1,0:T(8,128)(2,1)} %tokens_hbm.1, bf16[1024,512]{1,0:T(8,128)(2,1)} %codes_hbm.1, s32[2,1024]{1,0:T(2,128)} %bitcast.1, bf16[128,512]{1,0:T(8,128)(2,1)} %cotangent_hbm.1, f32[1,128]{1,0:T(1,128)} %constant.2.clone.inverse_hbm), custom_call_target="tpu_custom_call" | custom-call | tf_op jit(solution)/shard_map/pallas_call | solution.py:581
  32.1 1.1 %shard_map.77 = (bf16[128,512]{1,0:T(8,128)(2,1)}, bf16[128,4096]{1,0:T(8,128)(2,1)}, f32[128,512]{1,0:T(8,128)}) custom-call(bf16[128,512]{1,0:T(8,128)(2,1)S(1)} %get-tuple-element.6.refs_0_, bf16[128,4096]{1,0:T(8,128)(2,1)S(1)} %get-tuple-element.7.refs_1_, f32[128,512]{1,0:T(8,128)S(1)} %get-tuple-element.8.refs_2_), custom_call_target="tpu_custom_call" | custom-call | tf_op jit(solution)/shard_map/pallas_call | solution.py:624

commit v4 on v3

--- a/solution.py
+++ b/solution.py
@@ -135,7 +135,8 @@
 
 CORES = 2
 DEPTH = 4
-GROUPS = ('S1', 'P2z', 'P2z')
+GROUPS = (('S1', 'S1'), ('Q2z', 'Q2z'))
+OVER = ()
 ROUTES = {
     "S1": {
         (0, 0): ("x", {"z": (1, 0), "y": (0, 1)}),
@@ -149,23 +150,34 @@
         (1, 0): ("z", {}),
         (1, 1): ("z", {}),
     },
-    "P2z": {(0, 0): ("x", {"z": (1, 0)}), (1, 0): ("z", {})},
-    "P2y": {(0, 0): ("x", {"y": (0, 1)}), (0, 1): ("y", {})},
+    "Q2z": {
+        (0, 0): ("x", {"z": (1, 0)}),
+        (0, 1): ("x", {"z": (1, 1)}),
+        (1, 0): ("z", {}),
+        (1, 1): ("z", {}),
+    },
+    "Q2y": {
+        (0, 0): ("x", {"y": (0, 1)}),
+        (1, 0): ("x", {"y": (1, 1)}),
+        (0, 1): ("y", {}),
+        (1, 1): ("y", {}),
+    },
 }
+KEYS = ((0, 0), (0, 1), (1, 0), (1, 1))
 SPLIT = 2
-PARTS = 2
-SIZES = {"S1": 4, "S2": 4, "P2z": 2, "P2y": 2}
+PARTS = len(GROUPS[0])
 ORDER = (
-    "exp", "bar", "xw1:00", "yc3f", "xw0:00", "deq", "trg", "ypre",
-    "cw", "yc2n", "yc3n", "xw2:00", "w1:00.0", "ccols", "yc2f", "yc1f",
-    "cpre", "o3", "o0", "yc1n", "w1:00.1", "yc0f", "w0:00.0", "rpre",
-    "w0:00.1", "g3f", "g2n", "w2:00.0", "v0:00", "u1:00", "v1:00", "w1:10.0",
-    "w0:10.0", "w2:00.1", "g2f", "g3n", "u0:00", "s00", "g1f", "w0:10.1",
-    "p0", "s01", "o2", "u2:00", "v0:10", "w2:10.1", "p1", "s10",
-    "yc0n", "g0f", "p2", "g1n", "w1:10.1", "s11", "s20", "w0:01.1",
-    "w2:10.0", "u2:10", "w0:01.0", "u0:10", "v1:10", "u0:01", "s21", "u1:10",
-    "w0:11.1", "v2:10", "w0:11.0", "p3", "g0n", "o1", "v0:11", "v0:01",
-    "u0:11", "v2:00", "key", "fin",
+    "exp", "bar", "yc3f", "xw1:01.0", "xw0:00.0", "xw1:01.1", "trg", "ypre",
+    "yc2f", "deq", "xw1:00.1", "ccols", "w1:01.0", "yc3n", "yc2n", "w0:00.0",
+    "xw0:00.1", "cpre", "yc1f", "rpre", "w1:01.1", "yc0f", "g3f", "xw1:00.0",
+    "yc1n", "cw", "w1:00.1", "o2", "w0:00.1", "g2f", "p0", "g3n",
+    "w0:10.0", "g2n", "s00e", "u0:00", "s01e", "p1", "g1f", "w1:11.0",
+    "w0:10.1", "w1:10.1", "s00i", "o0", "w1:00.0", "s10e", "v1:01", "o1",
+    "yc0n", "s01i", "g0f", "s11e", "w0:01.0", "g1n", "u1:00", "u1:01",
+    "p3", "s20e", "s10i", "s20i", "w1:11.1", "s11i", "s21i", "w1:10.0",
+    "s21e", "o3", "w0:11.0", "u1:10", "p2", "w0:01.1", "w0:11.1", "v0:10",
+    "u1:11", "g0n", "v0:00", "u0:11", "v1:10", "u0:01", "v1:00", "u0:10",
+    "v0:11", "v0:01", "v1:11", "key", "fin",
 )
 
 
@@ -217,7 +229,7 @@
     row_count = columns.shape[2]
     shard_rows = weights.shape[1]
     features = pre.shape[1]
-    unit_rows = shard_rows // sum(SIZES[g] for g in GROUPS)
+    unit_rows = shard_rows // (len(KEYS) * len(GROUPS))
     part_rows = unit_rows // PARTS
     width = features // SPLIT
     total = count * nodes * locals_
@@ -253,20 +265,14 @@
 
     zbit = lax.rem(depth_at, 2)
     ybit = lax.rem(node, 2)
-    bases = [sum(SIZES[g] for g in GROUPS[:i]) for i in range(len(GROUPS))]
 
     def unit_first(group, key):
-        kind = GROUPS[group]
-        dz, dy = key
-        zz = 1 - zbit if dz else zbit
-        yy = 1 - ybit if dy else ybit
-        index = {"S1": 2 * zz + yy, "S2": 2 * zz + yy, "P2z": zz, "P2y": yy}[kind]
-        return pl.multiple_of((bases[group] + index) * unit_rows, unit_rows)
+        zz = 1 - zbit if key[0] else zbit
+        yy = 1 - ybit if key[1] else ybit
+        return pl.multiple_of((len(KEYS) * group + 2 * zz + yy) * unit_rows, unit_rows)
 
     def sem_index(group, key):
-        kind = GROUPS[group]
-        dz, dy = key
-        return bases[group] + {"S1": 2 * dz + dy, "S2": 2 * dz + dy, "P2z": dz, "P2y": dy}[kind]
+        return len(KEYS) * group + 2 * key[0] + key[1]
 
     def load(source, target, at):
         copy = pltpu.make_async_copy(source, target, load_sem.at[at])
@@ -275,8 +281,10 @@
 
     load_exponents = load(exponents_hbm, exponents_ref, 0)
     load_codes = {}
-    keys = [(g, key) for g in range(len(GROUPS)) for key in ROUTES[GROUPS[g]]]
-    first_keys = [(g, key) for g, key in keys if ROUTES[GROUPS[g]][key][0] == "x"]
+    keys = [(g, key) for g in range(len(GROUPS)) for key in KEYS]
+    first_keys = [
+        (g, key) for g, key in keys if any(ROUTES[kind][key][0] == "x" for kind in GROUPS[g])
+    ]
     rest_keys = [pair for pair in keys if pair not in first_keys]
 
     def start_codes(pairs):
@@ -343,10 +351,20 @@
             device_id_type=MESH,
         )
 
-    def send(src, dst, send_sem, recv_sem, peer):
+    inner_sends = []
+
+    def send(src, dst, send_sem, recv_sem, peer, only=None):
         copy = describe(src, dst, send_sem, recv_sem, peer)
-        copy.start()
-        sends.append(copy)
+        if only is None:
+            copy.start()
+            sends.append(copy)
+        else:
+            only.append(copy)
+
+            @pl.when(inner == 1)
+            def _():
+                copy.start()
+
         return copy
 
     def send_columns(name, slot, peer, r, far, e, d):
@@ -389,13 +407,15 @@
     def send_unit(source, slot, group, source_key, key, part, peer):
         first = unit_first(group, source_key) + part * part_rows
         rows = pl.ds(pl.multiple_of(first, part_rows), part_rows)
-        lane_of = {"x": 0, "y": 1, "z": 2, "c": 3}[peer]
+        lane_of = {"x": 0, "y": 1, "z": 2, "c": 3, "m": 4}[peer]
+        only = inner_sends if peer in "zm" and (group, part, source_key) in OVER else None
         waits["w", slot, group, key, part] = send(
             weights.at[source, rows, :],
             weights.at[slot, rows, :],
             weight_send.at[lane_of, sem_index(group, source_key), part],
             weight_recv.at[slot - 2, sem_index(group, key), part],
             peer,
+            only,
         )
 
     def piece(r, far):
@@ -421,8 +441,8 @@
                 )
     order_of = ((3, 2, 1), (2, 3, 1))
 
-    def chain(i, k):
-        for middle in range(2):
+    def chain(i, k, places):
+        for middle in places:
 
             @pl.when(inner == middle)
             def _():
@@ -493,8 +513,7 @@
             send_columns("d", 3, "d", r, far, 1, 1)
         elif head[:2] == "xw":
             group, key = int(head[2:]), (int(rest[0]), int(rest[1]))
-            for part in range(PARTS):
-                send_unit(0, 2, group, key, key, part, "x")
+            send_unit(0, 2, group, key, key, int(rest[3]), "x")
         elif head[0] == "o":
             use(0, int(head[1]) * block_rows, block_rows)
         elif head[0] == "p":
@@ -504,8 +523,10 @@
             group, key = int(head[1:]), (int(rest[0]), int(rest[1]))
             part = int(rest[3])
             waits["w", 2, group, key, part].wait_recv()
-            for peer, there in ROUTES[GROUPS[group]][key][1].items():
+            for peer, there in ROUTES[GROUPS[group][part]][key][1].items():
                 send_unit(2, 2, group, key, there, part, peer)
+                if peer == "z" and (group, part, key) in OVER:
+                    send_unit(2, 2, group, key, there, part, "m")
             send_unit(2, 3, group, key, key, part, "c")
         elif head[0] in "uv":
             group, key = int(head[1:]), (int(rest[0]), int(rest[1]))
@@ -531,7 +552,7 @@
             else:
                 kept[r] = value
         elif head[0] == "s":
-            chain(int(head[1]), int(head[2]))
+            chain(int(head[1]), int(head[2]), ("ei".index(head[3]),))
         elif step == "key":
             keys_ref[...] = turn(projected[...], rotation[0], rotation[1]).astype(jnp.bfloat16)
         elif step == "fin":
@@ -549,6 +570,12 @@
         run(step)
     for copy in sends:
         copy.wait_send()
+
+    @pl.when(inner == 1)
+    def _():
+        for copy in inner_sends:
+            copy.wait_send()
+
     for middle in range(2):
 
         @pl.when(inner == middle)
@@ -572,7 +599,7 @@
     count, width = tokens.shape
     shard_rows, features = key_codes.shape
     row_count = width // (nodes * locals_)
-    units = sum(SIZES[g] for g in GROUPS)
+    units = len(KEYS) * len(GROUPS)
     half = THETA ** (-(np.arange(HEAD // 2) * 2.0 / HEAD))
     inverse = jnp.asarray(np.concatenate([half, half])[None, :], jnp.float32)
     anywhere = pl.BlockSpec(memory_space=pl.ANY)
@@ -612,7 +639,7 @@
             dma((4,)),
             dma((4,)),
             dma((4,)),
-            dma((4, units, PARTS)),
+            dma((5, units, PARTS)),
             dma((2, units, PARTS)),
             dma((DEPTH * SPLIT,)),
             dma((DEPTH * SPLIT,)),

time: 33.4 us -> 32.8 us (0.982)
  Pallas kernels: 32.5 us -> 31.9 us
    pallas_call x1, Pallas kernels: 31.4 us -> 30.8 us  [fused(): pl.pallas_call(fused_kernel, out_shape=(pltpu.VMEM((count, features), jnp...]
where the time goes in v4:
time: 32.8 us; the launch traced here: 32.6 us
  Pallas kernels  31.9 us (97%)
  between operations  0.64 us (2%)
    pallas_call x1, Pallas kernels, fused(): pl.pallas_call(fused_kernel, out_shape=(pltpu.VMEM((count, features), jnp...  30.8 us
    pallas_call x1, Pallas kernels, fused(): pl.pallas_call(place, out_shape=tuple((jax.ShapeDtypeStruct(a.shape, a.dt...  1.12 us

profile of v4, /device:TPU:0, one launch (start us, length us, event | category | flops | bytes accessed | tf_op | source)
XLA Modules:
  0.0 32.6 jit_solution(17904423498336296312)
XLA Ops:
  0.6 30.8 %shard_map.76 = (bf16[128,512]{1,0:T(8,128)(2,1)S(1)}, bf16[128,4096]{1,0:T(8,128)(2,1)S(1)}, f32[128,512]{1,0:T(8,128)S(1)}) custom-call(bf16[128,4096]{1,0:T(8,128)(2,1)} %tokens_hbm.1, bf16[1024,512]{1,0:T(8,128)(2,1)} %codes_hbm.1, s32[2,1024]{1,0:T(2,128)} %bitcast.1, bf16[128,512]{1,0:T(8,128)(2,1)} %cotangent_hbm.1, f32[1,128]{1,0:T(1,128)} %constant.2.clone.inverse_hbm), custom_call_target="tpu_custom_call" | custom-call | tf_op jit(solution)/shard_map/pallas_call | solution.py:608
  31.5 1.1 %shard_map.77 = (bf16[128,512]{1,0:T(8,128)(2,1)}, bf16[128,4096]{1,0:T(8,128)(2,1)}, f32[128,512]{1,0:T(8,128)}) custom-call(bf16[128,512]{1,0:T(8,128)(2,1)S(1)} %get-tuple-element.6.refs_0_, bf16[128,4096]{1,0:T(8,128)(2,1)S(1)} %get-tuple-element.7.refs_1_, f32[128,512]{1,0:T(8,128)S(1)} %get-tuple-element.8.refs_2_), custom_call_target="tpu_custom_call" | custom-call | tf_op jit(solution)/shard_map/pallas_call | solution.py:651

commit v5 on v4

--- a/solution.py
+++ b/solution.py
@@ -136,7 +136,7 @@
 CORES = 2
 DEPTH = 4
 GROUPS = (('S1', 'S1'), ('Q2z', 'Q2z'))
-OVER = ()
+OVER = ((0, 0, (0, 0)), (0, 1, (0, 0)), (1, 0, (0, 0)), (1, 1, (0, 0)))
 ROUTES = {
     "S1": {
         (0, 0): ("x", {"z": (1, 0), "y": (0, 1)}),
@@ -167,17 +167,17 @@
 SPLIT = 2
 PARTS = len(GROUPS[0])
 ORDER = (
-    "exp", "bar", "yc3f", "xw1:01.0", "xw0:00.0", "xw1:01.1", "trg", "ypre",
-    "yc2f", "deq", "xw1:00.1", "ccols", "w1:01.0", "yc3n", "yc2n", "w0:00.0",
-    "xw0:00.1", "cpre", "yc1f", "rpre", "w1:01.1", "yc0f", "g3f", "xw1:00.0",
-    "yc1n", "cw", "w1:00.1", "o2", "w0:00.1", "g2f", "p0", "g3n",
-    "w0:10.0", "g2n", "s00e", "u0:00", "s01e", "p1", "g1f", "w1:11.0",
-    "w0:10.1", "w1:10.1", "s00i", "o0", "w1:00.0", "s10e", "v1:01", "o1",
-    "yc0n", "s01i", "g0f", "s11e", "w0:01.0", "g1n", "u1:00", "u1:01",
-    "p3", "s20e", "s10i", "s20i", "w1:11.1", "s11i", "s21i", "w1:10.0",
-    "s21e", "o3", "w0:11.0", "u1:10", "p2", "w0:01.1", "w0:11.1", "v0:10",
-    "u1:11", "g0n", "v0:00", "u0:11", "v1:10", "u0:01", "v1:00", "u0:10",
-    "v0:11", "v0:01", "v1:11", "key", "fin",
+    "exp", "bar", "xw1:00.0", "trg", "ypre", "xw1:01.1", "deq", "cpre",
+    "cw", "xw0:00.0", "yc3f", "xw0:00.1", "p3", "w1:00.0", "yc2f", "p1",
+    "ccols", "yc3n", "yc1f", "xw1:00.1", "p2", "w1:01.1", "rpre", "g3f",
+    "yc2n", "p0", "yc0f", "yc1n", "g2f", "g3n", "w0:00.0", "s00e",
+    "w0:00.1", "u0:00", "s01e", "o3", "w1:00.1", "g2n", "xw1:01.0", "g1f",
+    "s10e", "w0:10.0", "s00i", "s11e", "w0:10.1", "v1:00", "g0f", "w1:10.0",
+    "s01i", "w1:01.0", "yc0n", "v0:00", "g1n", "w1:10.1", "w1:11.1", "o2",
+    "s20e", "s10i", "s20i", "o1", "w0:01.0", "w0:01.1", "v1:01", "s21e",
+    "s11i", "s21i", "u1:01", "u1:00", "v0:10", "w1:11.0", "u0:10", "u1:11",
+    "v1:10", "w0:11.0", "u0:01", "u1:10", "o0", "w0:11.1", "u0:11", "v1:11",
+    "v0:01", "v0:11", "key", "g0n", "fin",
 )
 
 

time: 32.8 us -> 31.6 us (0.963)
  Pallas kernels: 31.9 us -> 30.8 us
    pallas_call x1, Pallas kernels: 30.8 us -> 29.6 us  [fused(): pl.pallas_call(fused_kernel, out_shape=(pltpu.VMEM((count, features), jnp...]
where the time goes in v5:
time: 31.6 us; the launch traced here: 31.4 us
  Pallas kernels  30.8 us (97%)
  between operations  0.64 us (2%)
    pallas_call x1, Pallas kernels, fused(): pl.pallas_call(fused_kernel, out_shape=(pltpu.VMEM((count, features), jnp...  29.6 us
    pallas_call x1, Pallas kernels, fused(): pl.pallas_call(place, out_shape=tuple((jax.ShapeDtypeStruct(a.shape, a.dt...  1.12 us

profile of v5, /device:TPU:0, one launch (start us, length us, event | category | flops | bytes accessed | tf_op | source)
XLA Modules:
  0.0 31.4 jit_solution(15010629584455923005)
XLA Ops:
  0.6 29.6 %shard_map.76 = (bf16[128,512]{1,0:T(8,128)(2,1)S(1)}, bf16[128,4096]{1,0:T(8,128)(2,1)S(1)}, f32[128,512]{1,0:T(8,128)S(1)}) custom-call(bf16[128,4096]{1,0:T(8,128)(2,1)} %tokens_hbm.1, bf16[1024,512]{1,0:T(8,128)(2,1)} %codes_hbm.1, s32[2,1024]{1,0:T(2,128)} %bitcast.1, bf16[128,512]{1,0:T(8,128)(2,1)} %cotangent_hbm.1, f32[1,128]{1,0:T(1,128)} %constant.2.clone.inverse_hbm), custom_call_target="tpu_custom_call" | custom-call | tf_op jit(solution)/shard_map/pallas_call | solution.py:608
  30.3 1.1 %shard_map.77 = (bf16[128,512]{1,0:T(8,128)(2,1)}, bf16[128,4096]{1,0:T(8,128)(2,1)}, f32[128,512]{1,0:T(8,128)}) custom-call(bf16[128,512]{1,0:T(8,128)(2,1)S(1)} %get-tuple-element.6.refs_0_, bf16[128,4096]{1,0:T(8,128)(2,1)S(1)} %get-tuple-element.7.refs_1_, f32[128,512]{1,0:T(8,128)S(1)} %get-tuple-element.8.refs_2_), custom_call_target="tpu_custom_call" | custom-call | tf_op jit(solution)/shard_map/pallas_call | solution.py:651
